TPU v7x, 32 devices: a whole 2x2x4 slice. The times are simulated.
32 devices in a mesh: dp: 8 (over z, core), col: 4 (over y, x).
Axes of the slice: x: 2, y: 2, z: 4, core: 2. Of those that a mesh axis runs over, the one named last changes fastest.
Arguments:
- features: bfloat16 [12288, 256], P(('dp', 'col')), may hold values from -6 to 6
- w_in: bfloat16 [256, 1024], replicated, may hold values from -0.375 to 0.375
- w_out: bfloat16 [1024, 64], replicated, may hold values from -0.1875 to 0.1875
- length_inv: float32 [64], replicated, may hold values from 0.2 to 0.6
- cg_vectors: bfloat16 [12288, 8], P(('dp', 'col')), may hold values from -6 to 6
- cotangent: bfloat16 [12288, 8], P(('dp', 'col')), may hold values from -6 to 6
Outputs:
- product: float32 [12288, 8], P(('dp', 'col'))
- grad_in: float32 [256, 1024], replicated
- grad_out: float32 [1024, 64], replicated
All inputs are finite; a program needn't handle non-finite values.
Results may differ from a plain program's by a relative error of at most 0.03.
Values may be sent and summed in bfloat16 or wider, within the bound.
A program may use at most 64 MiB of HBM per device.

v0:
```python
import math

import jax
import jax.numpy as jnp
from jax import lax
from jax.sharding import PartitionSpec as P


def pair_block(zrow, sqrow, crow, zcol, sqcol, vcol, mixed):
    f32 = jnp.float32
    inner = (((1,), (1,)), ((), ()))
    cross = lax.dot_general(zrow, zcol, inner, preferred_element_type=f32)
    kern = jnp.exp(-0.5 * (sqrow[:, None] + sqcol[None, :] - 2.0 * cross)).astype(jnp.bfloat16)
    prod = jnp.dot(kern, vcol, preferred_element_type=f32)
    pair = lax.dot_general(crow, mixed, inner, preferred_element_type=f32)
    spair = (pair * kern.astype(f32)).astype(jnp.bfloat16)
    acc = jnp.dot(spair, zcol, preferred_element_type=f32)
    rsum = jnp.sum(spair.astype(f32), axis=1)
    return (prod, acc, rsum)


def tile_sums(carry, rows, piece):
    zrow, sqrow, crow = rows
    zcol, vcol, ccol = piece
    width = zrow.shape[1]
    sqcol = jnp.sum(jnp.square(zcol.astype(jnp.float32)), axis=1)
    mixed = jnp.concatenate([vcol, ccol], axis=1)
    count = zcol.shape[0]
    col_block = count if count <= 4096 else math.gcd(count, 4096)
    nrows = zrow.shape[0]
    row_block = math.gcd(nrows, 512)
    row_count = nrows // row_block
    row_parts = (
        zrow.reshape(row_count, row_block, width),
        sqrow.reshape(row_count, row_block),
        crow.reshape(row_count, row_block, crow.shape[1]),
    )

    def step(total, cols):
        zcb, sqcb, vcb, mcb = cols

        def one_rows(block_rows):
            return pair_block(block_rows[0], block_rows[1], block_rows[2], zcb, sqcb, vcb, mcb)

        prod, acc, rsum = lax.map(one_rows, row_parts)
        return (
            (
                total[0] + prod.reshape(nrows, -1),
                total[1] + acc.reshape(nrows, width),
                total[2] + rsum.reshape(nrows),
            ),
            None,
        )

    col_count = count // col_block
    col_parts = (
        zcol.reshape(col_count, col_block, width),
        sqcol.reshape(col_count, col_block),
        vcol.reshape(col_count, col_block, vcol.shape[1]),
        mixed.reshape(col_count, col_block, mixed.shape[1]),
    )
    result, _ = lax.scan(step, carry, col_parts)
    return result


def start_rows(zrow, vrow, crow_in):
    zf = zrow.astype(jnp.float32)
    return (zrow, jnp.sum(zf * zf, axis=1), jnp.concatenate([crow_in, vrow], axis=1))


def empty_sums(nrows, rhs, width):
    return (
        jnp.zeros((nrows, rhs), jnp.float32),
        jnp.zeros((nrows, width), jnp.float32),
        jnp.zeros((nrows,), jnp.float32),
    )


def local(features, w_in, w_out, length_inv, cg_vectors, cotangent):
    f32 = jnp.float32
    pre = jnp.dot(features, w_in, preferred_element_type=f32)
    hidden = jax.nn.silu(pre).astype(jnp.bfloat16)
    embed = jnp.dot(hidden, w_out, preferred_element_type=f32).astype(jnp.bfloat16)
    scaled = (embed.astype(f32) * length_inv).astype(jnp.bfloat16)
    rhs = cg_vectors.shape[1]
    width = scaled.shape[1]
    zrow, vrow, crow_in = (
        lax.all_gather(scaled, "col", axis=0, tiled=True),
        lax.all_gather(cg_vectors, "col", axis=0, tiled=True),
        lax.all_gather(cotangent, "col", axis=0, tiled=True),
    )
    rows = start_rows(zrow, vrow, crow_in)
    prod, acc, rsum = tile_sums(
        empty_sums(zrow.shape[0], rhs, width),
        rows,
        (
            lax.all_gather(scaled, "dp", axis=0, tiled=True),
            lax.all_gather(cg_vectors, "dp", axis=0, tiled=True),
            lax.all_gather(cotangent, "dp", axis=0, tiled=True),
        ),
    )
    partial_grad = acc - rsum[:, None] * zrow.astype(f32)
    product, grad_scaled = (
        lax.psum_scatter(prod.astype(jnp.bfloat16), "col", scatter_dimension=0, tiled=True).astype(
            jnp.float32
        ),
        lax.psum_scatter(
            partial_grad.astype(jnp.bfloat16), "col", scatter_dimension=0, tiled=True
        ).astype(jnp.float32),
    )
    grad_embed = (grad_scaled * length_inv).astype(jnp.bfloat16)
    over_rows = (((0,), (0,)), ((), ()))
    part_out = lax.dot_general(hidden, grad_embed, over_rows, preferred_element_type=f32)
    dhid = lax.dot_general(grad_embed, w_out, (((1,), (1,)), ((), ())), preferred_element_type=f32)
    sig = jax.nn.sigmoid(pre)
    grad_pre = (dhid * sig * (1.0 + pre * (1.0 - sig))).astype(jnp.bfloat16)
    part_in = lax.dot_general(features, grad_pre, over_rows, preferred_element_type=f32)
    grad_in, grad_out = lax.psum((part_in, part_out), ("dp", "col"))
    return (product, grad_in, grad_out)


def solution(mesh):
    placed = (P(("dp", "col"), None), P(), P(), P(), P(("dp", "col"), None), P(("dp", "col"), None))
    return jax.shard_map(
        local,
        mesh=mesh,
        in_specs=placed,
        out_specs=(P(("dp", "col"), None), P(), P()),
        check_vma=False,
    )
```

profile of v0, /device:TPU:0, one launch (start us, length us, event | category | flops | bytes accessed | tf_op | source)
XLA Modules:
  0.0 309.4 jit_solution(6096048379735893209)
XLA Ops:
  7.2 9.9 %all_gather.22 = bf16[1536,8]{0,1:T(8,128)(2,1)S(1)} all-gather(bf16[384,8]{0,1:T(8,128)(2,1)} %param.12), channel_id=1, replica_groups=mesh['dp'=8,'col'=4] {'col'}, dimensions={0}, use_global_device_ids=true | all-gather | bytes 30720 | tf_op jit(solution)/shard_map/all_gather | solution.py:89
  17.1 14.4 %all_gather.20 = bf16[3072,8]{0,1:T(8,128)(2,1)S(1)} all-gather(bf16[384,8]{0,1:T(8,128)(2,1)} %param.12), channel_id=1, replica_groups=mesh['dp'=8,'col'=4] {'dp'}, dimensions={0}, use_global_device_ids=true | all-gather | bytes 55296 | tf_op jit(solution)/shard_map/all_gather | solution.py:98
  31.5 8.0 %all_gather.21 = bf16[1536,8]{0,1:T(8,128)(2,1)S(1)} all-gather(bf16[384,8]{0,1:T(8,128)(2,1)} %param.13), channel_id=1, replica_groups=mesh['dp'=8,'col'=4] {'col'}, dimensions={0}, use_global_device_ids=true | all-gather | bytes 30720 | tf_op jit(solution)/shard_map/all_gather | solution.py:90
  39.5 14.2 %all_gather.23 = bf16[3072,8]{0,1:T(8,128)(2,1)S(1)} all-gather(bf16[384,8]{0,1:T(8,128)(2,1)} %param.13), channel_id=1, replica_groups=mesh['dp'=8,'col'=4] {'dp'}, dimensions={0}, use_global_device_ids=true | all-gather | bytes 55296 | tf_op jit(solution)/shard_map/all_gather | solution.py:99
  53.7 2.6 multiply_convert_fusion.2
  56.4 0.4 fusion.9
  56.7 8.1 %all_gather.18 = bf16[1536,64]{0,1:T(8,128)(2,1)S(1)} all-gather(bf16[384,64]{0,1:T(8,128)(2,1)S(1)} %fusion.9), channel_id=1, replica_groups=mesh['dp'=8,'col'=4] {'col'}, dimensions={0}, use_global_device_ids=true | all-gather | bytes 245760 | tf_op jit(solution)/shard_map/all_gather | solution.py:88
  64.9 14.5 %all_gather.19 = bf16[3072,64]{0,1:T(8,128)(2,1)S(1)} all-gather(bf16[384,64]{0,1:T(8,128)(2,1)S(1)} %fusion.9), channel_id=1, replica_groups=mesh['dp'=8,'col'=4] {'dp'}, dimensions={0}, use_global_device_ids=true | all-gather | bytes 442368 | tf_op jit(solution)/shard_map/all_gather | solution.py:97
  79.4 0.7 multiply_reduce_fusion
  80.1 0.4 copy.19
  80.6 0.2 copy.23
  80.9 26.3 %while.25 = (s32[]{:T(128)}, bf16[3,512,8]{1,2,0:T(8,128)(2,1)}, f32[3,512,64]{1,0,2:T(4,128)S(1)}, f32[3,512]{1,0:T(4,128)}, f32[3,512]{1,0:T(4,128)S(1)}, /*in...) while((s32[]{:T(128)}, bf16[3,512,8]{1,2,0:T(8,128)(2,1)}, ...), condition=%wide.region_4.5_spmd, body=%wide.region_2.4_spmd.sunk | while | flops 493878784 | bytes 17899676 | solution.py:45
  80.9 2.3 exponential_convert_fusion.2
  83.2 1.5 fusion.44
  84.7 1.1 convert_reduce_fusion.2
  85.8 1.1 convolution_bitcast_fusion.4
  86.9 0.1 copy.37
  87.1 1.3 dynamic_update_slice.18
  88.4 1.2 dynamic_update_slice.17
  89.7 2.3 exponential_convert_fusion.2
  92.0 1.5 fusion.44
  93.5 1.1 convert_reduce_fusion.2
  94.6 1.1 convolution_bitcast_fusion.4
  95.7 0.1 copy.37
  95.9 1.3 dynamic_update_slice.18
  97.2 1.2 dynamic_update_slice.17
  98.4 2.3 exponential_convert_fusion.2
  100.8 1.5 fusion.44
  102.3 1.1 convert_reduce_fusion.2
  103.4 1.1 convolution_bitcast_fusion.4
  104.5 0.1 copy.37
  104.6 1.3 dynamic_update_slice.18
  106.0 1.2 dynamic_update_slice.17
  107.2 0.8 mul.53
  108.0 0.1 copy.33
  108.1 0.1 fusion.13
  108.2 0.9 copy.26
  109.2 1.7 copy.24
  110.9 23.0 %reduce-scatter.9.cloned.1.call-done = bf16[384,64]{1,0:T(8,128)(2,1)} async-done(((bf16[1536,64]{1,0:T(8,128)(2,1)}), bf16[384,64]{1,0:T(8,128)(2,1)}) %reduce-scatter.9.cloned.1.call-update) | async-done | bytes 49168
  133.9 1.0 copy.27
  134.9 3.5 %convolution_bitcast_fusion.2 = f32[256,1024]{0,1:T(8,128)} fusion(bf16[384,256]{1,0:T(8,128)(2,1)S(1)} %copy-done.4, f32[384,1024]{1,0:T(8,128)} %get-tuple-element.167, bf16[1024,64]{0,1:T(8,128)(2,1)S(1)} %copy-done.2, bf16[384,64]{0,1:T(8,128)(2,1)S(1)} %copy.27, f32[64]{0:T(128)S(1)} %copy-done.3), kind=kOutput, calls=%fused_computation.16 | convolution fusion | flops 255270912 | bytes 2998528 | tf_op jit(solution)/shard_map/dot_general | solution.py:117
  138.3 1.0 fusion.14
  139.4 21.7 %reduce-scatter.7.cloned.1.call-done = bf16[384,8]{1,0:T(8,128)(2,1)} async-done(((bf16[1536,8]{1,0:T(8,128)(2,1)}), bf16[384,8]{1,0:T(8,128)(2,1)}) %reduce-scatter.7.cloned.1.call-update) | async-done | bytes 6160
  161.1 1.0 copy.25
  162.1 0.6 convert_element_type.60
  162.7 136.0 %all-reduce.3.cloned.1.call-done = (f32[256,1024]{0,1:T(8,128)}, f32[1024,64]{0,1:T(8,128)}) async-done(((f32[256,1024]{0,1:T(8,128)}, f32[1024,64]{0,1:T(8,128)}), (f32[256,1024]{0,1:T(8,128)}, f32[1024,64]{0,1:T(8,128)})) %all-reduce.3.cloned.1.call-update) | async-done | bytes 1310736 | tf_op jit(solution)/shard_map/psum | solution.py:118
  298.6 2.5 copy.22
  301.2 1.7 copy.55
  (27 shorter events, 0.3 us)
Async XLA Ops:
  7.2 46.6 %copy-start = (bf16[256,1024]{1,0:T(8,128)(2,1)S(1)}, bf16[256,1024]{1,0:T(8,128)(2,1)}, u32[]{:S(2)}) copy-start(bf16[256,1024]{1,0:T(8,128)(2,1)} %param.9) | copy-start | bytes 1572868
  7.2 126.7 %reduce-scatter.9.cloned.1.call-start = ((), (), s32[]{:S(2)}) async-start(), calls=%async_computation.3 | async-start | bytes 491520
  53.7 2.6 copy-start.1
  53.7 2.6 copy-start.3
  107.2 27.6 %copy-start.2 = (bf16[1024,64]{0,1:T(8,128)(2,1)S(1)}, bf16[1024,64]{0,1:T(8,128)(2,1)}, u32[]{:S(2)}) copy-start(bf16[1024,64]{0,1:T(8,128)(2,1)} %param.10) | copy-start | bytes 393220
  107.2 27.6 %copy-start.4 = (bf16[384,256]{1,0:T(8,128)(2,1)S(1)}, bf16[384,256]{1,0:T(8,128)(2,1)}, u32[]{:S(2)}) copy-start(bf16[384,256]{1,0:T(8,128)(2,1)} %param.8) | copy-start | bytes 589828
  109.1 52.0 %reduce-scatter.7.cloned.1.call-start = ((), (), s32[]{:S(2)}) async-start(), calls=%async_computation.2 | async-start | bytes 491520
  110.8 187.8 %all-reduce.3.cloned.1.call-start = ((), (), s32[]{:S(2)}) async-start(), calls=%async_computation.4 | async-start | bytes 2621440 | tf_op jit(solution)/shard_map/psum | solution.py:118
Sparse Core Ops, SparseCore 0:
  109.2 24.5 reduce-scatter.8
  136.6 24.4 reduce-scatter.6
  167.1 131.5 all-reduce.2
where the time goes:
time: 310 us; the launch traced here: 309 us
  waiting for transfers between devices  181 us (58%)
  blocking collectives  69.2 us (22%)
  matrix products  25.6 us (8%)
  local copies, waits for them, and re-layouts  18.3 us (6%)
  between operations  13.9 us (4%)
    psum x1, waiting for transfers between devices, local(): grad_in, grad_out = lax.psum((part_in, part_out), ('dp', 'col'))  136 us
    unnamed x5, waiting for transfers between devices  44.7 us
    all_gather x1, blocking collectives, local(): lax.all_gather(scaled, 'dp', axis=0, tiled=True)  14.5 us
    all_gather x1, blocking collectives, local(): lax.all_gather(cg_vectors, 'dp', axis=0, tiled=True)  14.4 us
    all_gather x1, blocking collectives, local(): lax.all_gather(cotangent, 'dp', axis=0, tiled=True)  14.2 us
    all_gather x1, blocking collectives, local(): lax.all_gather(cg_vectors, 'col', axis=0, tiled=True)  9.88 us
    unnamed x17, local copies, waits for them, and re-layouts  8.87 us
    all_gather x1, blocking collectives, local(): lax.all_gather(scaled, 'col', axis=0, tiled=True)  8.15 us
  transfers between devices with their start and end apart: 3, of which 3 were waited for; matrix products, arithmetic and copies ran while one was open for 3% of the time, Pallas kernels for 0%

commit v1 on v0

v1 whole, which is shorter than its diff:
```python
import functools

import jax
import jax.numpy as jnp
from jax import lax
from jax.experimental import pallas as pl
from jax.experimental.pallas import tpu as pltpu
from jax.sharding import PartitionSpec as P

MESH = pl.DeviceIdType.MESH
f32 = jnp.float32
bf16 = jnp.bfloat16
LANES = 128
SUB = 16


def iota(shape, dim):
    return lax.broadcasted_iota(jnp.int32, shape, dim)


def dot(a, b, ca=1, cb=0):
    return lax.dot_general(a, b, (((ca,), (cb,)), ((), ())), preferred_element_type=f32)


def kernel(n_dp, n_col, tp, feat, w_in, w_out, linv, vec, cot, prod_o, gin_o, gout_o,
           hid, der, rows_s, cols_s, et, pt, sv, sz, acc, msg, part, gbuf, hbuf, rbuf, pbuf, fbuf,
           row_send, row_recv, col_send, col_recv, fwd_send, msg_send, msg_recv,
           core_send, core_recv, rs_send, rs_recv, ag_send, ag_recv):
    m, width = feat.shape[0], w_out.shape[1]
    rhs = vec.shape[1]
    hidden_units = w_in.shape[1]
    features_n = feat.shape[1]
    nz = n_dp // 2
    n2 = nz * n_col
    half = n2 * tp
    dp = lax.axis_index("dp")
    col = lax.axis_index("col")
    z = dp // 2
    core = dp - 2 * z
    mate = (2 * z + 1 - core, col)
    me2 = z * n_col + col

    def peer(k):
        q = lax.rem(me2 + k, n2)
        return q, (2 * (q // n_col) + core, lax.rem(q, n_col))

    barrier = pltpu.get_barrier_semaphore()
    pl.semaphore_signal(barrier, inc=1, device_id=mate, device_id_type=MESH)

    @pl.loop(1, n2)
    def _(k):
        pl.semaphore_signal(barrier, inc=1, device_id=peer(k)[1], device_id_type=MESH)

    pre = dot(feat[...], w_in[...])
    sig = 1.0 / (1.0 + jnp.exp(-pre))
    hid[...] = (pre * sig).astype(bf16)
    der[...] = sig * (1.0 + pre * (1.0 - sig))
    embed = dot(hid[...], w_out[...]).astype(bf16)
    scaled = (embed.astype(f32) * linv[...]).astype(bf16)
    zf = scaled.astype(f32)
    nh = -0.5 * jnp.sum(zf * zf, axis=1, keepdims=True)
    t0 = nh.astype(bf16).astype(f32)
    t1 = (nh - t0).astype(bf16).astype(f32)
    t2 = (nh - t0 - t1).astype(bf16).astype(f32)
    vat, cat, sat = width, width + rhs, width + 2 * rhs
    one = sat + 3

    def place(value, at):
        n = value.shape[1]
        sel = (iota((n, LANES), 1) == iota((n, LANES), 0) + at).astype(f32).astype(bf16)
        return dot(value, sel)

    lane = iota((m, LANES), 1)
    block = place(scaled, 0) + place(vec[...], vat) + place(cot[...], cat)
    block = jnp.where(lane == sat, t0, block)
    block = jnp.where(lane == sat + 1, t1, block)
    block = jnp.where(lane == sat + 2, t2, block)
    block = jnp.where((lane >= one) & (lane < one + 3), 1.0, block)
    block = block.astype(bf16)
    rows_s[col] = block
    cols_s[dp] = block

    pl.semaphore_wait(barrier, n2)

    def row_copy(to, slot):
        return pltpu.make_async_remote_copy(
            src_ref=rows_s.at[col], dst_ref=rows_s.at[slot], send_sem=row_send.at[to],
            recv_sem=row_recv.at[slot], device_id=(dp, to), device_id_type=MESH)

    def col_copy(to, slot):
        return pltpu.make_async_remote_copy(
            src_ref=cols_s.at[dp], dst_ref=cols_s.at[slot], send_sem=col_send.at[to],
            recv_sem=col_recv.at[slot], device_id=(to, col), device_id_type=MESH)

    def fwd_copy(slot):
        return pltpu.make_async_remote_copy(
            src_ref=cols_s.at[slot], dst_ref=cols_s.at[slot], send_sem=fwd_send.at[slot // 2],
            recv_sem=col_recv.at[slot], device_id=mate, device_id_type=MESH)

    def msg_copy(to, slot):
        return pltpu.make_async_remote_copy(
            src_ref=msg.at[to], dst_ref=part.at[slot], send_sem=msg_send.at[to],
            recv_sem=msg_recv.at[slot], device_id=(dp, to), device_id_type=MESH)

    col_copy(2 * z + 1 - core, dp).start()

    @pl.loop(1, nz)
    def _(k):
        col_copy(2 * lax.rem(z + k, nz) + core, dp).start()

    @pl.loop(1, n_col)
    def _(j):
        row_copy(lax.rem(col + j, n_col), col).start()

    acc[...] = jnp.zeros_like(acc)
    a, b = iota((2 * LANES, LANES), 0), iota((2 * LANES, LANES), 1)
    want = jnp.where(a < width, a, -1)
    want = jnp.where((a >= sat) & (a < one), a + 3, want)
    want = jnp.where((a >= one) & (a < one + 3), a - 3, want)
    low = a - LANES
    want = jnp.where((low >= vat) & (low < cat), low + rhs, want)
    want = jnp.where((low >= cat) & (low < sat), low - rhs, want)
    perm = (want == b).astype(f32).astype(bf16)
    keep_v = (lane >= vat) & (lane < cat)
    keep_z = (lane < width) | (lane == one)

    def prepare(zz):
        for side in range(2):
            blk = cols_s[2 * zz + side]
            ep = dot(perm, blk, 1, 1).astype(bf16)
            at = slice(side * m, (side + 1) * m)
            et[zz, :, at] = ep[:LANES]
            pt[zz, :, at] = ep[LANES:]
            wide = blk.astype(f32)
            sv[zz, at, :] = jnp.where(keep_v, wide, 0.0).astype(bf16)
            sz[zz, at, :] = jnp.where(keep_z, wide, 0.0).astype(bf16)

    def finish(chunk):
        total = acc[chunk]
        zrow = jnp.where(lane < width, rows_s[chunk].astype(f32), 0.0)
        return total - total[:, one:one + 1] * zrow

    @pl.loop(0, nz)
    def _(k):
        zz = lax.rem(z + k, nz)
        col_copy(dp, 2 * zz + 1 - core).wait_recv()
        prepare(zz)

        @pl.loop(0, n_col)
        def _(j):
            chunk = lax.rem(col + j + jnp.where(k == 0, 0, 1), n_col)

            @pl.when((k == 0) & (j > 0))
            def _():
                row_copy(col, chunk).wait_recv()

            lhs = rows_s[chunk]
            kern = jnp.exp(dot(lhs, et[zz]))
            pair = dot(lhs, pt[zz])
            kb = kern.astype(bf16)
            sp = (pair * kb.astype(f32)).astype(bf16)
            acc[chunk] += dot(kb, sv[zz]) + dot(sp, sz[zz])

            @pl.when((j == 0) & (k < nz - 1))
            def _():
                slot = 2 * lax.rem(z + k + 1, nz) + core
                col_copy(dp, slot).wait_recv()
                fwd_copy(slot).start()

            @pl.when((k == nz - 1) & (j < n_col - 1))
            def _():
                msg[chunk] = finish(chunk).astype(bf16)
                msg_copy(chunk, col).start()

    total = finish(col)
    for j in range(1, n_col):
        src = lax.rem(col + j, n_col)
        msg_copy(col, src).wait_recv()
        total = total + part[src].astype(f32)
    prod_o[...] = total[:, vat:cat]

    grad_embed = (total[:, :width] * linv[...]).astype(bf16)
    grad_pre = (dot(grad_embed, w_out[...], 1, 1) * der[...]).astype(bf16)
    gin = dot(feat[...], grad_pre, 0, 0).astype(bf16)
    gout = dot(grad_embed, hid[...], 0, 0).astype(bf16)
    lgroups = hidden_units // LANES
    rgroups_in = features_n // SUB
    rgroups = rgroups_in + width // SUB
    for rg in range(rgroups):
        for lg in range(lgroups):
            at = slice(lg * LANES, (lg + 1) * LANES)
            if rg < rgroups_in:
                tile = gin[rg * SUB:(rg + 1) * SUB, at]
            else:
                r = rg - rgroups_in
                tile = gout[r * SUB:(r + 1) * SUB, at]
            gbuf[rg * lgroups + lg] = tile
    used = rgroups * lgroups
    if used < 2 * half:
        gbuf[used:] = jnp.zeros((2 * half - used, SUB, LANES), bf16)

    give = pltpu.make_async_remote_copy(
        src_ref=gbuf.at[pl.ds((1 - core) * half, half)], dst_ref=hbuf, send_sem=core_send.at[0],
        recv_sem=core_recv.at[0], device_id=mate, device_id_type=MESH)
    give.start()
    give.wait_recv()
    rbuf[...] = (gbuf[pl.ds(core * half, half)].astype(f32) + hbuf[...].astype(f32)).astype(bf16)

    def rs_copy(q, device, slot):
        return pltpu.make_async_remote_copy(
            src_ref=rbuf.at[pl.ds(q * tp, tp)], dst_ref=pbuf.at[slot], send_sem=rs_send.at[q],
            recv_sem=rs_recv.at[slot], device_id=device, device_id_type=MESH)

    @pl.loop(1, n2)
    def _(k):
        q, device = peer(k)
        rs_copy(q, device, me2).start()

    def add(k, so_far):
        q, device = peer(k)
        rs_copy(q, device, q).wait_recv()
        return so_far + pbuf[q].astype(f32)

    mine = lax.fori_loop(1, n2, add, rbuf[pl.ds(me2 * tp, tp)].astype(f32))
    home = core * half
    fbuf[pl.ds(home + me2 * tp, tp)] = mine.astype(bf16)

    def ag_copy(q, device, slot):
        return pltpu.make_async_remote_copy(
            src_ref=fbuf.at[pl.ds(home + me2 * tp, tp)],
            dst_ref=fbuf.at[pl.ds(home + slot * tp, tp)], send_sem=ag_send.at[q],
            recv_sem=ag_recv.at[slot], device_id=device, device_id_type=MESH)

    @pl.loop(1, n2)
    def _(k):
        q, device = peer(k)
        ag_copy(q, device, me2).start()

    @pl.loop(1, n2)
    def _(k):
        q, device = peer(k)
        ag_copy(q, device, q).wait_recv()

    share = pltpu.make_async_remote_copy(
        src_ref=fbuf.at[pl.ds(home, half)], dst_ref=fbuf.at[pl.ds(home, half)],
        send_sem=core_send.at[1], recv_sem=core_recv.at[1], device_id=mate, device_id_type=MESH)
    share.start()

    col_copy(2 * z + 1 - core, dp).wait_send()
    give.wait_send()

    @pl.loop(1, nz)
    def _(k):
        zz = lax.rem(z + k, nz)
        col_copy(2 * zz + core, dp).wait_send()
        fwd_copy(2 * zz + core).wait_send()

    @pl.loop(1, n_col)
    def _(j):
        to = lax.rem(col + j, n_col)
        row_copy(to, col).wait_send()
        msg_copy(to, col).wait_send()

    @pl.loop(1, n2)
    def _(k):
        q, device = peer(k)
        rs_copy(q, device, me2).wait_send()
        ag_copy(q, device, me2).wait_send()

    pltpu.make_async_remote_copy(
        src_ref=fbuf.at[pl.ds(home, half)], dst_ref=fbuf.at[pl.ds((1 - core) * half, half)],
        send_sem=core_send.at[1], recv_sem=core_recv.at[1], device_id=mate,
        device_id_type=MESH).wait_recv()
    for rg in range(rgroups):
        for lg in range(lgroups):
            at = slice(lg * LANES, (lg + 1) * LANES)
            tile = fbuf[rg * lgroups + lg].astype(f32)
            if rg < rgroups_in:
                gin_o[rg * SUB:(rg + 1) * SUB, at] = tile
            else:
                r = rg - rgroups_in
                gout_o[r * SUB:(r + 1) * SUB, at] = tile
    share.wait_send()


def local(n_dp, n_col, features, w_in, w_out, length_inv, cg_vectors, cotangent):
    m, feat_n = features.shape
    hidden_units, width = w_out.shape
    rhs = cg_vectors.shape[1]
    nz, n2 = n_dp // 2, n_dp // 2 * n_col
    tiles = (feat_n + width) // SUB * (hidden_units // LANES)
    tp = -(-tiles // (2 * n2))
    half = n2 * tp
    dma = pltpu.SemaphoreType.DMA
    vm = pltpu.VMEM
    product, gin, gout = pl.pallas_call(
        functools.partial(kernel, n_dp, n_col, tp),
        out_shape=(
            jax.ShapeDtypeStruct((m, rhs), f32),
            jax.ShapeDtypeStruct((feat_n, hidden_units), f32),
            jax.ShapeDtypeStruct((width, hidden_units), f32),
        ),
        in_specs=[pl.BlockSpec(memory_space=vm)] * 6,
        out_specs=(pl.BlockSpec(memory_space=vm),) * 3,
        scratch_shapes=[
            vm((m, hidden_units), bf16),
            vm((m, hidden_units), f32),
            vm((n_col, m, LANES), bf16),
            vm((n_dp, m, LANES), bf16),
            vm((nz, LANES, 2 * m), bf16),
            vm((nz, LANES, 2 * m), bf16),
            vm((nz, 2 * m, LANES), bf16),
            vm((nz, 2 * m, LANES), bf16),
            vm((n_col, m, LANES), f32),
            vm((n_col, m, LANES), bf16),
            vm((n_col, m, LANES), bf16),
            vm((2 * half, SUB, LANES), bf16),
            vm((half, SUB, LANES), bf16),
            vm((half, SUB, LANES), bf16),
            vm((n2, tp, SUB, LANES), bf16),
            vm((2 * half, SUB, LANES), bf16),
            dma((n_col,)), dma((n_col,)),
            dma((n_dp,)), dma((n_dp,)), dma((nz,)),
            dma((n_col,)), dma((n_col,)),
            dma((2,)), dma((2,)),
            dma((n2,)), dma((n2,)), dma((n2,)), dma((n2,)),
        ],
        compiler_params=pltpu.CompilerParams(
            collective_id=0, has_side_effects=True, vmem_limit_bytes=48 << 20
        ),
    )(features, w_in, w_out, length_inv.reshape(1, width), cg_vectors, cotangent)
    return product, gin, gout.T


def solution(mesh):
    placed = (P(("dp", "col"), None), P(), P(), P(), P(("dp", "col"), None), P(("dp", "col"), None))
    return jax.shard_map(
        functools.partial(local, mesh.shape["dp"], mesh.shape["col"]),
        mesh=mesh,
        in_specs=placed,
        out_specs=(P(("dp", "col"), None), P(), P()),
        check_vma=False,
    )
```

time: 310 us -> 59.5 us (0.19)
  waiting for transfers between devices: 181 us -> 0 us
  blocking collectives: 69.2 us -> 0 us
  Pallas kernels: 0 us -> 51.8 us
  matrix products: 25.6 us -> 0 us
  between operations: 13.9 us -> 0.69 us
  local copies, waits for them, and re-layouts: 18.3 us -> 6.15 us
    psum x1 -> x0, waiting for transfers between devices: 136 us -> none  [local(): grad_in, grad_out = lax.psum((part_in, part_out), ('dp', 'col'))]
    all_gather x6 -> x0, blocking collectives: 69.2 us -> none  [the longest x1 14.5 us: local(): lax.all_gather(scaled, 'dp', axis=0, tiled=True)]
    pallas_call x0 -> x1, Pallas kernels: none -> 51.8 us  [local(): pl.pallas_call(functools.partial(kernel, n_dp, n_col, tp), out_shape=(jax...]
    unnamed x5 -> x0, waiting for transfers between devices: 44.7 us -> none
    dot_general x16 -> x0, matrix products: 25.6 us -> none  [the longest x3 6.91 us: pair_block(): cross = lax.dot_general(zrow, zcol, inner, preferred_element_type=f32)]
    dynamic_update_slice x9 -> x0, local copies, waits for them, and re-layouts: 8.08 us -> none  [step(): prod, acc, rsum = lax.map(one_rows, row_parts)]
    unnamed x17 -> x12, local copies, waits for them, and re-layouts: 8.87 us -> 6.15 us
  transfers between devices with their start and end apart: 3 -> 0, of which waited for: 3 -> 0; matrix products, arithmetic and copies ran while one was open for 3% -> 0% of each run, Pallas kernels for 0% -> 0%
where the time goes in v1:
time: 59.5 us; the launch traced here: 58.6 us
  Pallas kernels  51.8 us (87%)
  local copies, waits for them, and re-layouts  6.15 us (10%)
  between operations  0.69 us (1%)
    pallas_call x1, Pallas kernels, local(): pl.pallas_call(functools.partial(kernel, n_dp, n_col, tp), out_shape=(jax...  51.8 us
    unnamed x12, local copies, waits for them, and re-layouts  6.15 us

profile of v1, /device:TPU:0, one launch (start us, length us, event | category | flops | bytes accessed | tf_op | source)
XLA Modules:
  0.0 58.6 jit_solution(16965916712587964809)
XLA Ops:
  0.6 0.0 copy-start
  0.6 0.9 %copy.10.vec = bf16[384,8]{1,0:T(8,128)(2,1)S(1)} copy(bf16[384,8]{0,1:T(8,128)(2,1)} %param.10) | data formatting | bytes 12288 | tf_op args[4]
  1.5 0.9 %copy.11.cot = bf16[384,8]{1,0:T(8,128)(2,1)S(1)} copy(bf16[384,8]{0,1:T(8,128)(2,1)} %param.11) | data formatting | bytes 12288 | tf_op args[5]
  2.4 0.0 copy-start.2
  2.4 1.1 %copy.9.w_out = bf16[1024,64]{1,0:T(8,128)(2,1)S(1)} copy(bf16[1024,64]{0,1:T(8,128)(2,1)} %param.8) | data formatting | bytes 262144 | tf_op args[2]
  3.5 0.0 copy-done
  3.5 0.0 copy-done.2
  3.5 0.0 copy-start.1
  3.5 0.9 %copy-done.1 = bf16[384,256]{1,0:T(8,128)(2,1)S(1)} copy-done((bf16[384,256]{1,0:T(8,128)(2,1)S(1)}, bf16[384,256]{1,0:T(8,128)(2,1)}, u32[]{:S(2)}) %copy-start.1) | copy-done | bytes 196632
  4.5 51.8 %shard_map.85 = (f32[384,8]{1,0:T(8,128)S(1)}, f32[256,1024]{1,0:T(8,128)S(1)}, f32[64,1024]{1,0:T(8,128)S(1)}) custom-call(bf16[384,256]{1,0:T(8,128)(2,1)S(1)} %copy-done.1, bf16[256,1024]{1,0:T(8,128)(2,1)S(1)} %copy-done, bf16[1024,64]{1,0:T(8,128)(2,1)S(1)} %copy.9.w_out, f32[1,64]{1,0:T(1,128)S(1)} %bitcast.3, bf16[384,8]{1,0:T(8,128)(2,1)S(1)} %copy.10.vec, ...), custom_call_target="tpu_custom_call" | custom-call | tf_op jit(solution)/shard_map/pallas_call | solution.py:296
  56.2 0.7 %copy.12 = f32[384,8]{0,1:T(8,128)} copy(f32[384,8]{1,0:T(8,128)S(1)} %get-tuple-element.9) | data formatting | bytes 24576
  56.9 1.0 %copy.15 = f32[256,1024]{1,0:T(8,128)} copy(f32[256,1024]{1,0:T(8,128)S(1)} %get-tuple-element.16) | data formatting | bytes 2097152
  57.9 0.7 %copy.16 = f32[1024,64]{0,1:T(8,128)} copy(f32[1024,64]{0,1:T(8,128)S(1)} %bitcast.2) | data formatting | bytes 524288
Async XLA Ops:
  0.6 2.9 %copy-start = (bf16[256,1024]{1,0:T(8,128)(2,1)S(1)}, bf16[256,1024]{1,0:T(8,128)(2,1)}, u32[]{:S(2)}) copy-start(bf16[256,1024]{1,0:T(8,128)(2,1)} %w_in.1) | copy-start | bytes 1572868
  2.4 1.1 %copy-start.2 = (f32[64]{0:T(128)S(1)}, f32[64]{0:T(128)}, u32[]{:S(2)}) copy-start(f32[64]{0:T(128)} %param.9) | copy-start | bytes 772
  3.5 0.9 %copy-start.1 = (bf16[384,256]{1,0:T(8,128)(2,1)S(1)}, bf16[384,256]{1,0:T(8,128)(2,1)}, u32[]{:S(2)}) copy-start(bf16[384,256]{1,0:T(8,128)(2,1)} %feat.1) | copy-start | bytes 589828

commit v2 on v1

v2 whole, which is shorter than its diff:
```python
import functools

import jax
import jax.numpy as jnp
from jax import lax
from jax.experimental import pallas as pl
from jax.experimental.pallas import tpu as pltpu
from jax.sharding import PartitionSpec as P

MESH = pl.DeviceIdType.MESH
f32 = jnp.float32
bf16 = jnp.bfloat16
LANES = 128
SUB = 16


def iota(shape, dim):
    return lax.broadcasted_iota(jnp.int32, shape, dim)


def dot(a, b, ca=1, cb=0):
    return lax.dot_general(a, b, (((ca,), (cb,)), ((), ())), preferred_element_type=f32)


def kernel(n_dp, n_col, tp, feat_h, w_in_h, w_out_h, linv_h, vec_h, cot_h, prod_o, gin_o, gout_o,
           feat, w_in, w_out, linv, vec, cot, hid, der, feat_t, rows_t, rows_s, cols_t, et, pt, sv, sz,
           acc, msg, part, gbuf, hbuf, rbuf, xbuf, yout, yin, fbuf,
           in_sem, row_send, row_recv, line_send, col_recv, fwd_send, msg_send, msg_recv,
           core_send, core_recv, xy_send, xy_recv, z_send, z_recv,
           agz_send, agx_send, ag_recv, mate_send, mate_recv):
    loads = [
        pltpu.make_async_copy(src, dst, in_sem.at[i])
        for i, (src, dst) in enumerate([
            (feat_h, feat), (w_in_h, w_in), (w_out_h, w_out), (linv_h, linv), (vec_h, vec), (cot_h, cot)])
    ]
    for load in loads:
        load.start()
    m, width = feat.shape[0], w_out.shape[0]
    rhs = vec.shape[0]
    hidden_units = w_in.shape[1]
    features_n = feat.shape[1]
    nz = n_dp // 2
    n2 = nz * n_col
    half = n2 * tp
    dp = lax.axis_index("dp")
    col = lax.axis_index("col")
    z = dp // 2
    core = dp - 2 * z
    mate = (2 * z + 1 - core, col)
    zc = n_col * tp
    home = core * half

    def z_at(s):
        return lax.rem(z + s, nz)

    def col_at(j):
        return lax.rem(col + j, n_col)

    barrier = pltpu.get_barrier_semaphore()
    pl.semaphore_signal(barrier, inc=1, device_id=mate, device_id_type=MESH)

    @pl.loop(1, nz)
    def _(s):
        pl.semaphore_signal(barrier, inc=1, device_id=(2 * z_at(s) + core, col), device_id_type=MESH)

    @pl.loop(1, n_col)
    def _(j):
        pl.semaphore_signal(barrier, inc=1, device_id=(dp, col_at(j)), device_id_type=MESH)

    loads[0].wait()
    loads[1].wait()
    pre = dot(feat[...], w_in[...])
    sig = 1.0 / (1.0 + jnp.exp(-pre))
    hid[...] = (pre * sig).astype(bf16)
    der[...] = sig * (1.0 + pre * (1.0 - sig))
    for load in loads[2:]:
        load.wait()
    embed = dot(hid[...], w_out[...], 1, 1).astype(bf16)
    scaled = (embed.astype(f32) * linv[...]).astype(bf16)
    vat, cat, sat = width, width + rhs, width + 2 * rhs
    one = sat + 3
    pick = (iota((width, LANES), 1) == iota((width, LANES), 0)).astype(f32).astype(bf16)
    mine_t = jnp.concatenate(
        [dot(scaled, pick).T[:width], vec[...].astype(f32), cot[...].astype(f32)], axis=0).astype(bf16)
    rows_t[col] = mine_t
    cols_t[dp] = mine_t
    feat_t[...] = feat[...].T
    acc[...] = jnp.zeros_like(acc)

    pl.semaphore_wait(barrier, nz + n_col - 1)

    def row_copy(to, slot):
        return pltpu.make_async_remote_copy(
            src_ref=rows_t.at[col], dst_ref=rows_t.at[slot], send_sem=row_send.at[to],
            recv_sem=row_recv.at[slot], device_id=(dp, to), device_id_type=MESH)

    def line_copy(to, zi):
        slot = 2 * zi + core
        return pltpu.make_async_remote_copy(
            src_ref=cols_t.at[slot], dst_ref=cols_t.at[slot], send_sem=line_send.at[to],
            recv_sem=col_recv.at[slot], device_id=(2 * to + core, col), device_id_type=MESH)

    def fwd_copy(zi):
        slot = 2 * zi + core
        return pltpu.make_async_remote_copy(
            src_ref=cols_t.at[slot], dst_ref=cols_t.at[slot], send_sem=fwd_send.at[zi],
            recv_sem=col_recv.at[slot], device_id=mate, device_id_type=MESH)

    def from_mate(zi):
        slot = 2 * zi + 1 - core
        return pltpu.make_async_remote_copy(
            src_ref=cols_t.at[slot], dst_ref=cols_t.at[slot], send_sem=fwd_send.at[zi],
            recv_sem=col_recv.at[slot], device_id=mate, device_id_type=MESH)

    def msg_copy(to, slot):
        return pltpu.make_async_remote_copy(
            src_ref=msg.at[to], dst_ref=part.at[slot], send_sem=msg_send.at[to],
            recv_sem=msg_recv.at[slot], device_id=(dp, to), device_id_type=MESH)

    fwd_copy(z).start()

    both = jnp.minimum(z, nz - 1 - z)
    far = jnp.where(z < nz - 1 - z, 1, -1)

    def z_order(k):
        near = jnp.where(k % 2 == 1, (k + 1) // 2, -((k + 1) // 2))
        return z + jnp.where(k <= 2 * both, near, far * (k - both))

    @pl.loop(1, nz)
    def _(k):
        line_copy(z_order(k), z).start()

    @pl.loop(1, n_col)
    def _(j):
        row_copy(col_at(j), col).start()

    lane = iota((m, LANES), 1)
    sub_at = iota((LANES, m), 0)
    keep_v = (lane >= vat) & (lane < cat)
    keep_z = (lane < width) | (lane == one)

    def expand(block_t):
        wide = block_t.astype(f32)
        nh = -0.5 * jnp.sum(wide[:width] * wide[:width], axis=0, keepdims=True)
        t0 = nh.astype(bf16).astype(f32)
        t1 = (nh - t0).astype(bf16).astype(f32)
        t2 = (nh - t0 - t1).astype(bf16).astype(f32)
        rest = jnp.zeros((LANES - sat, m), f32)

        def tail(full, at_t, at_one):
            full = jnp.where(sub_at == at_t, t0, full)
            full = jnp.where(sub_at == at_t + 1, t1, full)
            full = jnp.where(sub_at == at_t + 2, t2, full)
            return jnp.where((sub_at >= at_one) & (sub_at < at_one + 3), 1.0, full)

        own = tail(jnp.concatenate([wide, rest], axis=0), sat, one)
        other = tail(jnp.concatenate([wide[:width], jnp.zeros((2 * rhs, m), f32), rest], axis=0), one, sat)
        swapped = jnp.concatenate(
            [jnp.zeros((width, m), f32), wide[cat:sat], wide[vat:cat], rest], axis=0)
        return own.T, other.astype(bf16), swapped.astype(bf16)

    def prepare(zz):
        for side in range(2):
            tall, other, swapped = expand(cols_t[2 * zz + side])
            at = slice(side * m, (side + 1) * m)
            et[zz, :, at] = other
            pt[zz, :, at] = swapped
            sv[zz, at, :] = jnp.where(keep_v, tall, 0.0).astype(bf16)
            sz[zz, at, :] = jnp.where(keep_z, tall, 0.0).astype(bf16)

    def tile(chunk, zz):
        lhs = rows_s[chunk]
        kern = jnp.exp(dot(lhs, et[zz]))
        pair = dot(lhs, pt[zz])
        kb = kern.astype(bf16)
        sp = (pair * kb.astype(f32)).astype(bf16)
        acc[chunk] += dot(kb, sv[zz]) + dot(sp, sz[zz])

    def finish(chunk):
        total = acc[chunk]
        zrow = jnp.where(lane < width, rows_s[chunk].astype(f32), 0.0)
        return (total - total[:, one:one + 1] * zrow).T[:sat]

    rows_s[col] = expand(mine_t)[0].astype(bf16)
    last = max(nz - 2, 1)

    @pl.loop(0, last)
    def _(k):
        zz = z_order(k)
        from_mate(zz).wait_recv()
        prepare(zz)

        @pl.loop(0, n_col)
        def _(j):
            chunk = col_at(j)

            @pl.when((k == 0) & (j > 0))
            def _():
                row_copy(col, chunk).wait_recv()
                rows_s[chunk] = expand(rows_t[chunk])[0].astype(bf16)

            tile(chunk, zz)
            t = k * n_col + j

            @pl.when((t % 2 == 1) & ((t + 1) // 2 < nz))
            def _():
                zi = z_order((t + 1) // 2)
                line_copy(zi, zi).wait_recv()
                fwd_copy(zi).start()

    @pl.loop(last, nz)
    def _(k):
        zz = z_order(k)
        from_mate(zz).wait_recv()
        prepare(zz)

    @pl.loop(0, n_col)
    def _(j):
        chunk = col_at(j + 1)

        @pl.loop(last, nz)
        def _(k):
            tile(chunk, z_order(k))

        @pl.when(j < n_col - 1)
        def _():
            msg[chunk] = finish(chunk).astype(bf16)
            msg_copy(chunk, col).start()

    total = finish(col)
    for j in range(1, n_col):
        src = lax.rem(col + j, n_col)
        msg_copy(col, src).wait_recv()
        total = total + part[src].astype(f32)
    prod_o[...] = total[vat:cat]

    square = (iota((width, width), 0) == iota((width, width), 1))
    scale = jnp.sum(jnp.where(square, linv[...], 0.0), axis=1, keepdims=True)
    grad_embed = (total[:width] * scale).astype(bf16)
    grad_pre = (dot(grad_embed, w_out[...], 0, 0) * der[...]).astype(bf16)
    gin = dot(feat_t[...], grad_pre).astype(bf16)
    gout = dot(grad_embed, hid[...]).astype(bf16)
    lgroups = hidden_units // LANES
    rgroups_in = features_n // SUB
    rgroups = rgroups_in + width // SUB
    for rg in range(rgroups):
        for lg in range(lgroups):
            at = slice(lg * LANES, (lg + 1) * LANES)
            if rg < rgroups_in:
                tile = gin[rg * SUB:(rg + 1) * SUB, at]
            else:
                r = rg - rgroups_in
                tile = gout[r * SUB:(r + 1) * SUB, at]
            gbuf[rg * lgroups + lg] = tile
    used = rgroups * lgroups
    if used < 2 * half:
        gbuf[used:] = jnp.zeros((2 * half - used, SUB, LANES), bf16)

    def swap_copy(zi):
        return pltpu.make_async_remote_copy(
            src_ref=gbuf.at[pl.ds((1 - core) * half + zi * zc, zc)], dst_ref=hbuf.at[pl.ds(zi * zc, zc)],
            send_sem=core_send.at[zi], recv_sem=core_recv.at[zi], device_id=mate, device_id_type=MESH)

    def xy_copy(zi, to, slot):
        return pltpu.make_async_remote_copy(
            src_ref=rbuf.at[pl.ds((zi * n_col + to) * tp, tp)], dst_ref=xbuf.at[zi, slot],
            send_sem=xy_send.at[zi, to], recv_sem=xy_recv.at[zi, slot],
            device_id=(dp, to), device_id_type=MESH)

    def z_copy(to, slot):
        return pltpu.make_async_remote_copy(
            src_ref=yout.at[to], dst_ref=yin.at[slot], send_sem=z_send.at[to], recv_sem=z_recv.at[slot],
            device_id=(2 * to + core, col), device_id_type=MESH)

    @pl.loop(0, nz)
    def _(s):
        swap_copy(z_at(s + 1)).start()

    @pl.loop(0, nz)
    def _(s):
        zi = z_at(s + 1)
        swap_copy(zi).wait_recv()
        here = pl.ds(zi * zc, zc)
        rbuf[here] = (gbuf[pl.ds(home + zi * zc, zc)].astype(f32) + hbuf[here].astype(f32)).astype(bf16)

        @pl.loop(1, n_col)
        def _(j):
            xy_copy(zi, col_at(j), col).start()

    def plane_sum(zi):
        def add(j, so_far):
            src = col_at(j)
            xy_copy(zi, src, src).wait_recv()
            return so_far + xbuf[zi, src].astype(f32)

        return lax.fori_loop(1, n_col, add, rbuf[pl.ds((zi * n_col + col) * tp, tp)].astype(f32))

    @pl.loop(0, nz - 1)
    def _(s):
        zi = z_at(s + 1)
        yout[zi] = plane_sum(zi).astype(bf16)
        z_copy(zi, z).start()

    def add_z(s, so_far):
        src = z_at(s)
        z_copy(src, src).wait_recv()
        return so_far + yin[src].astype(f32)

    mine = lax.fori_loop(1, nz, add_z, plane_sum(z))

    def piece(zi, ci):
        return fbuf.at[pl.ds(home + (zi * n_col + ci) * tp, tp)]

    def agz_copy(to, slot):
        return pltpu.make_async_remote_copy(
            src_ref=piece(slot, col), dst_ref=piece(slot, col), send_sem=agz_send.at[to],
            recv_sem=ag_recv.at[slot, col], device_id=(2 * to + core, col), device_id_type=MESH)

    def agx_copy(zi, to, slot):
        return pltpu.make_async_remote_copy(
            src_ref=piece(zi, slot), dst_ref=piece(zi, slot), send_sem=agx_send.at[zi, to],
            recv_sem=ag_recv.at[zi, slot], device_id=(dp, to), device_id_type=MESH)

    def mate_copy(zi, ci):
        return pltpu.make_async_remote_copy(
            src_ref=piece(zi, ci), dst_ref=piece(zi, ci), send_sem=mate_send.at[zi, ci],
            recv_sem=mate_recv.at[zi, ci], device_id=mate, device_id_type=MESH)

    fbuf[pl.ds(home + (z * n_col + col) * tp, tp)] = mine.astype(bf16)

    @pl.loop(1, nz)
    def _(s):
        agz_copy(z_at(s), z).start()

    @pl.loop(0, nz)
    def _(s):
        zi = z_at(s)

        @pl.when(s > 0)
        def _():
            agz_copy(zi, zi).wait_recv()

        @pl.loop(1, n_col)
        def _(j):
            agx_copy(zi, col_at(j), col).start()

        mate_copy(zi, col).start()

    @pl.loop(0, nz)
    def _(s):
        zi = z_at(s)

        @pl.loop(1, n_col)
        def _(j):
            src = col_at(j)
            agx_copy(zi, src, src).wait_recv()
            mate_copy(zi, src).start()

    fwd_copy(z).wait_send()

    @pl.loop(1, nz)
    def _(s):
        zz = z_at(s)
        line_copy(zz, z).wait_send()
        fwd_copy(zz).wait_send()
        z_copy(zz, z).wait_send()
        agz_copy(zz, z).wait_send()

    @pl.loop(1, n_col)
    def _(j):
        to = col_at(j)
        row_copy(to, col).wait_send()
        msg_copy(to, col).wait_send()

        @pl.loop(0, nz)
        def _(zi):
            xy_copy(zi, to, col).wait_send()
            agx_copy(zi, to, col).wait_send()

    @pl.loop(0, nz)
    def _(zi):
        swap_copy(zi).wait_send()

        @pl.loop(0, n_col)
        def _(ci):
            mate_copy(zi, ci).wait_send()

    @pl.loop(0, nz)
    def _(s):
        zi = z_at(s)

        @pl.loop(0, n_col)
        def _(j):
            ci = col_at(j)
            away = fbuf.at[pl.ds((1 - core) * half + (zi * n_col + ci) * tp, tp)]
            pltpu.make_async_remote_copy(
                src_ref=away, dst_ref=away, send_sem=mate_send.at[zi, ci],
                recv_sem=mate_recv.at[zi, ci], device_id=mate, device_id_type=MESH).wait_recv()

    for rg in range(rgroups):
        for lg in range(lgroups):
            at = slice(lg * LANES, (lg + 1) * LANES)
            tile_f = fbuf[rg * lgroups + lg].astype(f32)
            if rg < rgroups_in:
                gin_o[rg * SUB:(rg + 1) * SUB, at] = tile_f
            else:
                r = rg - rgroups_in
                gout_o[r * SUB:(r + 1) * SUB, at] = tile_f


def local(n_dp, n_col, features, w_in, w_out, length_inv, cg_vectors, cotangent):
    m, feat_n = features.shape
    hidden_units, width = w_out.shape
    rhs = cg_vectors.shape[1]
    nz, n2 = n_dp // 2, n_dp // 2 * n_col
    tiles = (feat_n + width) // SUB * (hidden_units // LANES)
    tp = -(-tiles // (2 * n2))
    half = n2 * tp
    dma = pltpu.SemaphoreType.DMA
    vm = pltpu.VMEM
    block = width + 2 * rhs
    product, gin, gout = pl.pallas_call(
        functools.partial(kernel, n_dp, n_col, tp),
        out_shape=(
            jax.ShapeDtypeStruct((rhs, m), f32),
            jax.ShapeDtypeStruct((feat_n, hidden_units), f32),
            jax.ShapeDtypeStruct((width, hidden_units), f32),
        ),
        in_specs=[pl.BlockSpec(memory_space=pltpu.HBM)] * 6,
        out_specs=(pl.BlockSpec(memory_space=vm),) * 3,
        scratch_shapes=[
            vm((m, feat_n), bf16),
            vm((feat_n, hidden_units), bf16),
            vm((width, hidden_units), bf16),
            vm((1, width), f32),
            vm((rhs, m), bf16),
            vm((rhs, m), bf16),
            vm((m, hidden_units), bf16),
            vm((m, hidden_units), f32),
            vm((feat_n, m), bf16),
            vm((n_col, block, m), bf16),
            vm((n_col, m, LANES), bf16),
            vm((n_dp, block, m), bf16),
            vm((nz, LANES, 2 * m), bf16),
            vm((nz, LANES, 2 * m), bf16),
            vm((nz, 2 * m, LANES), bf16),
            vm((nz, 2 * m, LANES), bf16),
            vm((n_col, m, LANES), f32),
            vm((n_col, block, m), bf16),
            vm((n_col, block, m), bf16),
            vm((2 * half, SUB, LANES), bf16),
            vm((half, SUB, LANES), bf16),
            vm((half, SUB, LANES), bf16),
            vm((nz, n_col, tp, SUB, LANES), bf16),
            vm((nz, tp, SUB, LANES), bf16),
            vm((nz, tp, SUB, LANES), bf16),
            vm((2 * half, SUB, LANES), bf16),
            dma((6,)), dma((n_col,)), dma((n_col,)),
            dma((nz,)), dma((n_dp,)), dma((nz,)),
            dma((n_col,)), dma((n_col,)),
            dma((nz,)), dma((nz,)),
            dma((nz, n_col)), dma((nz, n_col)),
            dma((nz,)), dma((nz,)),
            dma((nz,)), dma((nz, n_col)), dma((nz, n_col)),
            dma((nz, n_col)), dma((nz, n_col)),
        ],
        compiler_params=pltpu.CompilerParams(
            collective_id=0, has_side_effects=True, vmem_limit_bytes=60 << 20
        ),
    )(features, w_in, w_out.T, length_inv.reshape(1, width), cg_vectors.T, cotangent.T)
    return product.T, gin, gout.T


def solution(mesh):
    placed = (P(("dp", "col"), None), P(), P(), P(), P(("dp", "col"), None), P(("dp", "col"), None))
    return jax.shard_map(
        functools.partial(local, mesh.shape["dp"], mesh.shape["col"]),
        mesh=mesh,
        in_specs=placed,
        out_specs=(P(("dp", "col"), None), P(), P()),
        check_vma=False,
    )
```

time: 59.5 us -> 51.3 us (0.86); the launches traced: 58.6 us -> 51 us
  Pallas kernels: 51.8 us -> 46 us
  local copies, waits for them, and re-layouts: 6.15 us -> 4.36 us
    pallas_call x1, Pallas kernels: 51.8 us -> 46 us  [local(): pl.pallas_call(functools.partial(kernel, n_dp, n_col, tp), out_shape=(jax...]
    unnamed x12 -> x5, local copies, waits for them, and re-layouts: 6.15 us -> 4.36 us
where the time goes in v2:
time: 51.3 us; the launch traced here: 51 us
  Pallas kernels  46 us (90%)
  local copies, waits for them, and re-layouts  4.36 us (8%)
  between operations  0.64 us (1%)
    pallas_call x1, Pallas kernels, local(): pl.pallas_call(functools.partial(kernel, n_dp, n_col, tp), out_shape=(jax...  46 us
    unnamed x5, local copies, waits for them, and re-layouts  4.36 us

profile of v2, /device:TPU:0, one launch (start us, length us, event | category | flops | bytes accessed | tf_op | source)
XLA Modules:
  0.0 51.0 jit_solution(12742897030332999954)
XLA Ops:
  0.6 46.0 %shard_map.85 = (f32[8,384]{1,0:T(8,128)}, f32[256,1024]{1,0:T(8,128)}, f32[64,1024]{1,0:T(8,128)}) custom-call(bf16[384,256]{1,0:T(8,128)(2,1)} %feat_h.1, bf16[256,1024]{1,0:T(8,128)(2,1)} %w_in_h.1, bf16[64,1024]{1,0:T(8,128)(2,1)} %bitcast.7, f32[1,64]{1,0:T(1,128)} %bitcast.11, bf16[8,384]{1,0:T(8,128)(2,1)} %bitcast.9, bf16[8,384]{1,0:T(8,128)(2,1)} %bitcast.10), custom_call_target="tpu_custom_call" | custom-call | tf_op jit(solution)/shard_map/pallas_call | solution.py:422
  46.7 1.3 %copy.12 = f32[384,8]{0,1:T(8,128)} copy(f32[384,8]{0,1:T(8,128)} %bitcast.8) | data formatting | bytes 24576
  48.0 0.0 copy-start
  48.0 2.3 %copy.13 = f32[256,1024]{1,0:T(8,128)} copy(f32[256,1024]{1,0:T(8,128)} %get-tuple-element.13) | data formatting | bytes 2097152
  50.3 0.0 copy-done
  50.3 0.7 %copy.14 = f32[1024,64]{0,1:T(8,128)} copy(f32[1024,64]{0,1:T(8,128)S(1)} %bitcast.6) | data formatting | bytes 524288
Async XLA Ops:
  48.0 2.4 %copy-start = (f32[64,1024]{1,0:T(8,128)S(1)}, f32[64,1024]{1,0:T(8,128)}, u32[]{:S(2)}) copy-start(f32[64,1024]{1,0:T(8,128)} %get-tuple-element.8) | copy-start | bytes 786436

commit v3 on v2

--- a/solution.py
+++ b/solution.py
@@ -400,7 +400,7 @@
     for rg in range(rgroups):
         for lg in range(lgroups):
             at = slice(lg * LANES, (lg + 1) * LANES)
-            tile_f = fbuf[rg * lgroups + lg].astype(f32)
+            tile_f = fbuf[rg * lgroups + lg]
             if rg < rgroups_in:
                 gin_o[rg * SUB:(rg + 1) * SUB, at] = tile_f
             else:
@@ -423,8 +423,8 @@
         functools.partial(kernel, n_dp, n_col, tp),
         out_shape=(
             jax.ShapeDtypeStruct((rhs, m), f32),
-            jax.ShapeDtypeStruct((feat_n, hidden_units), f32),
-            jax.ShapeDtypeStruct((width, hidden_units), f32),
+            jax.ShapeDtypeStruct((feat_n, hidden_units), bf16),
+            jax.ShapeDtypeStruct((width, hidden_units), bf16),
         ),
         in_specs=[pl.BlockSpec(memory_space=pltpu.HBM)] * 6,
         out_specs=(pl.BlockSpec(memory_space=vm),) * 3,
@@ -468,7 +468,7 @@
             collective_id=0, has_side_effects=True, vmem_limit_bytes=60 << 20
         ),
     )(features, w_in, w_out.T, length_inv.reshape(1, width), cg_vectors.T, cotangent.T)
-    return product.T, gin, gout.T
+    return product.T, gin.astype(f32), gout.astype(f32).T
 
 
 def solution(mesh):

time: 51.3 us -> 50.2 us (0.979)
  local copies, waits for them, and re-layouts: 4.36 us -> 0.61 us
  other arithmetic: 0 us -> 2.88 us
    unnamed x5, local copies, waits for them, and re-layouts: 4.36 us -> 0.61 us
    convert_element_type x0 -> x1, other arithmetic: none -> 2.16 us  [local(): return (product.T, gin.astype(f32), gout.astype(f32).T)]
    transpose x0 -> x1, other arithmetic: none -> 0.72 us  [local(): return (product.T, gin.astype(f32), gout.astype(f32).T)]
where the time goes in v3:
time: 50.2 us; the launch traced here: 50 us
  Pallas kernels  45.8 us (91%)
  other arithmetic  2.88 us (6%)
  between operations  0.65 us (1%)
  local copies, waits for them, and re-layouts  0.61 us (1%)
    pallas_call x1, Pallas kernels, local(): pl.pallas_call(functools.partial(kernel, n_dp, n_col, tp), out_shape=(jax...  45.8 us
    convert_element_type x1, other arithmetic, local(): return (product.T, gin.astype(f32), gout.astype(f32).T)  2.16 us

profile of v3, /device:TPU:0, one launch (start us, length us, event | category | flops | bytes accessed | tf_op | source)
XLA Modules:
  0.0 50.0 jit_solution(4913547122212368939)
XLA Ops:
  0.6 45.8 %shard_map.85 = (f32[8,384]{1,0:T(8,128)}, bf16[256,1024]{1,0:T(8,128)(2,1)}, bf16[64,1024]{1,0:T(8,128)(2,1)}) custom-call(bf16[384,256]{1,0:T(8,128)(2,1)} %feat_h.1, bf16[256,1024]{1,0:T(8,128)(2,1)} %w_in_h.1, bf16[64,1024]{1,0:T(8,128)(2,1)} %bitcast.7, f32[1,64]{1,0:T(1,128)} %bitcast.11, bf16[8,384]{1,0:T(8,128)(2,1)} %bitcast.9, bf16[8,384]{1,0:T(8,128)(2,1)} %bitcast.10), custom_call_target="tpu_custom_call" | custom-call | tf_op jit(solution)/shard_map/pallas_call | solution.py:422
  46.5 0.0 copy-start
  46.5 2.2 %convert_element_type.4 = f32[256,1024]{1,0:T(8,128)} convert(bf16[256,1024]{1,0:T(8,128)(2,1)} %get-tuple-element.7) | non-fusion elementwise | flops 262144 | bytes 1572864 | tf_op jit(solution)/shard_map/convert_element_type | solution.py:471
  48.6 0.0 copy-done
  48.6 0.0 copy-start.1
  48.6 0.7 %convert_bitcast_fusion = f32[1024,64]{0,1:T(8,128)} fusion(bf16[64,1024]{1,0:T(8,128)(2,1)S(1)} %copy-done), kind=kLoop, calls=%fused_computation | loop fusion | flops 65536 | bytes 393216 | tf_op jit(solution)/shard_map/transpose | solution.py:471
  49.4 0.0 copy-done.1
  49.4 0.6 %copy.10 = f32[384,8]{0,1:T(8,128)} copy(f32[384,8]{0,1:T(8,128)S(1)} %bitcast.8) | data formatting | bytes 24576
Async XLA Ops:
  46.5 2.2 %copy-start = (bf16[64,1024]{1,0:T(8,128)(2,1)S(1)}, bf16[64,1024]{1,0:T(8,128)(2,1)}, u32[]{:S(2)}) copy-start(bf16[64,1024]{1,0:T(8,128)(2,1)} %get-tuple-element.8) | copy-start | bytes 393220
  48.6 0.7 %copy-start.1 = (f32[8,384]{1,0:T(8,128)S(1)}, f32[8,384]{1,0:T(8,128)}, u32[]{:S(2)}) copy-start(f32[8,384]{1,0:T(8,128)} %get-tuple-element.6) | copy-start | bytes 36868
